TPU v7x, 32 devices: a whole 2x2x4 slice. The times are simulated.
32 devices in a mesh: row: 8 (over z, x), col: 4 (over y, core).
Axes of the slice: x: 2, y: 2, z: 4, core: 2. Of those that a mesh axis runs over, the one named last changes fastest.
Arguments:
- diagonal_inverses: bfloat16 [24, 2048, 2048], P('row', 'col'), may hold values from -0.125 to 0.125
- column_basis: bfloat16 [24, 2048, 256], P('row', 'col'), may hold values from -6 to 6
- row_basis: bfloat16 [24, 2048, 256], P('row', 'col'), may hold values from -0.125 to 0.125
- transfer: float32 [24, 256, 256], P('row', 'col'), may hold values from -0.375 to 0.375
- coupling: float32 [24, 256, 256], P('row', 'col'), may hold values from -6 to 6
- ranks: int32 [24], P('row'), may hold values from 128 to 256, as said below
Outputs:
- merged: float32 [24, 256, 256], P('row', 'col')
- parent_skeleton: float32 [24, 256, 256], P('row', 'col')
Inputs may be any that keep to these rules, and one draw needn't show every extreme that they name: `ranks`: each rank is 128 or 256; both occur in every draw.
All inputs are finite; a program needn't handle non-finite values.
Results may differ from a plain program's by a relative error of at most 0.0021.
Values may be sent and summed in bfloat16 or wider, within the bound.
A program may use at most 64 MiB of HBM per device.

v0:
```python
import jax
import jax.numpy as jnp
from jax import lax
from jax.experimental import pallas as pl
from jax.experimental.pallas import tpu as pltpu
from jax.sharding import PartitionSpec as P

BIT = 2
MESH = pl.DeviceIdType.MESH
LY, LC, LF, TY, TC, TF, TZ, TG, ZC, ZG, SC, SY, PC, PY, PZ, MY, MF = range(17)


def kernel(
    ranks_ref, d_ref, l_ref, r_ref, t_ref, k_ref, out_ref,
    dv, lv, rv, tv, kv, tw, zw, sbuf, sgot, ysend, ygot, pbuf, pgot, pysend, pygot, qsend, qgot,
    esend, egot, mv, pv, send_sem, recv_sem, d_sem, loc_sem, out_sem,
):
    nodes, block, _ = l_ref.shape
    part = t_ref.shape[1]
    width = t_ref.shape[2]
    c = lax.axis_index("col")
    r = lax.axis_index("row")
    core = lax.rem(c, 2)
    y = lax.div(c, 2)
    cp = c + 1 - 2 * core
    yp = c + 2 - 4 * y
    high = lax.rem(lax.div(r, 1 << BIT), 2)
    sib = r + (1 << BIT) - (2 << BIT) * high
    other = 1 - y

    to_core = {"col": cp}
    to_y = {"col": yp}
    to_z = {"row": sib}
    slots = (c, cp, yp, cp + yp - c)

    def halves(x):
        top = x.astype(jnp.bfloat16)
        return top, (x - top.astype(jnp.float32)).astype(jnp.bfloat16)

    def product(a, b, dims):
        a_top, a_low = halves(a)
        b_top, b_low = halves(b)
        lhs = jnp.concatenate([a_top, a_low, a_top], axis=dims[0])
        rhs = jnp.concatenate([b_top, b_top, b_low], axis=dims[1])
        return lax.dot_general(
            lhs, rhs, (((dims[0],), (dims[1],)), ((), ())), preferred_element_type=jnp.float32
        )

    def rows_of(index):
        return pl.ds(pl.multiple_of(index * part, part), part)

    t_in = pltpu.make_async_copy(t_ref, tv, loc_sem.at[0])
    t_in.start()
    barrier = pltpu.get_barrier_semaphore()
    for device in (to_core, to_y, to_z):
        pl.semaphore_signal(barrier, inc=1, device_id=device, device_id_type=MESH)

    row_at = lax.broadcasted_iota(jnp.int32, (part, width), 0) + c * part
    col_at = lax.broadcasted_iota(jnp.int32, (part, width), 1)
    l_in, d_in = [], []
    for n in range(nodes):
        cp_l = pltpu.make_async_copy(l_ref.at[n], lv.at[n, pl.ds(0, block)], d_sem.at[n, 4])
        cp_l.start()
        l_in.append(cp_l)
        for s in range(4):
            src = d_ref.at[n, :, pl.ds(pl.multiple_of(slots[s] * block, block), block)]
            one = pltpu.make_async_copy(src, dv.at[n, :, pl.ds(s * block, block)], d_sem.at[n, s])
            one.start()
            d_in.append(one)
    r_in = pltpu.make_async_copy(r_ref, rv, loc_sem.at[1])
    r_in.start()
    k_in = pltpu.make_async_copy(k_ref, kv, loc_sem.at[2])
    k_in.start()
    t_in.wait()
    for n in range(nodes):
        tw[n, rows_of(c), :] = jnp.where(row_at < ranks_ref[n], tv[n], 0.0)
    pl.semaphore_wait(barrier, 3)

    sent = []

    def copy(kind, n, src, dst, device):
        return pltpu.make_async_remote_copy(
            src_ref=src, dst_ref=dst, send_sem=send_sem.at[kind, n], recv_sem=recv_sem.at[kind, n],
            device_id=device, device_id_type=MESH,
        )

    def send(kind, n, src, dst, device):
        one = copy(kind, n, src, dst, device)
        one.start()
        sent.append(one)

    def got(kind, n, ref, device):
        copy(kind, n, ref, ref, device).wait_recv()

    def slot(n, s):
        return lv.at[n, pl.ds(s * block, block)]

    def strip(buf, n, index):
        return buf.at[n, rows_of(index)]

    half = block // 2
    rest = block - half
    last = nodes - 1

    def piece(n, s, first):
        return lv.at[n, pl.ds(s * block + first, rest if first else half)]

    def send_basis(n):
        send(LY, n, l_ref.at[n], slot(n, 2), to_y)

    for n in range(nodes):
        send(TY, n, strip(tw, n, c), strip(tw, n, c), to_y)
        send(TZ, n, strip(tw, n, c), strip(zw, n, c), to_z)
        send(TC, n, strip(tw, n, c), strip(tw, n, c), to_core)
    for n in range(nodes):
        if n < last:
            send_basis(n)
        send(LC, n, l_ref.at[n], slot(n, 1), to_core)
    def times(n, first, size):
        span = pl.ds(first, size)
        return jnp.dot(dv[n, :, span], lv[n, span, :], preferred_element_type=jnp.float32)

    def relay(n):
        got(TY, n, strip(tw, n, yp), to_y)
        send(TG, n, strip(tw, n, yp), strip(zw, n, yp), to_z)
        send(TF, n, strip(tw, n, yp), strip(tw, n, yp), to_core)

    def begin(n):
        l_in[n].wait()
        for s in range(4):
            d_in[4 * n + s].wait()
        got(LC, n, slot(n, 1), to_core)
        return times(n, 0, 2 * block)

    def eliminate(n):
        total = begin(n)
        got(LY, n, slot(n, 2), to_y)
        send(LF, n, slot(n, 2), slot(n, 3), to_core)
        total = total + times(n, 2 * block, block)
        got(LF, n, slot(n, 3), to_core)
        total = total + times(n, 3 * block, block)
        skeletons(n, total)

    def skeletons(n, total):
        skeleton = lax.dot_general(
            rv[n], total.astype(jnp.bfloat16), (((0,), (0,)), ((), ())), preferred_element_type=jnp.float32
        )
        sbuf[n] = skeleton.reshape(2, 2, part, width)
        send(SC, n, sbuf.at[n, :, 1 - core], sgot.at[n], to_core)

    def reduce_chip(n):
        got(SC, n, sgot.at[n], to_core)
        ysend[n] = (sbuf[n, other, core] + sgot[n, other]).astype(ysend.dtype)
        send(SY, n, ysend.at[n], ygot.at[n], to_y)

    def couple(n):
        got(ZC, n, strip(zw, n, cp), to_core)
        got(ZG, n, strip(zw, n, slots[3]), to_core)
        got(TC, n, strip(tw, n, cp), to_core)
        got(TF, n, strip(tw, n, slots[3]), to_core)
        mv[n] = product(kv[n], zw[n], (1, 0))

    outs = []

    def merge(n):
        got(SY, n, ygot.at[n], to_y)
        mine = sbuf[n, y, core] + sgot[n, y] + ygot[n].astype(jnp.float32)
        live = (row_at < ranks_ref[n]) & (col_at < ranks_ref[n])
        mine = jnp.where(live, mine, 0.0)
        merged = mv[n] + product(mine, tw[n], (1, 0))
        mv[n] = merged
        own = product(tw[n, rows_of(c), :], merged, (0, 0))
        pbuf[n] = own.reshape(2, 2, part, width)
        send(PC, n, pbuf.at[n, :, 1 - core], pgot.at[n], to_core)
        one = pltpu.make_async_copy(mv.at[n], out_ref.at[0, n], out_sem.at[0, n])
        one.start()
        outs.append(one)

    def parent_chip(n):
        got(PC, n, pgot.at[n], to_core)
        over = pbuf[n, other, core] + pgot[n, other]
        if n < last:
            pysend[n] = over
            send(PY, n, pysend.at[n], pygot.at[n], to_y)
        else:
            qsend[...] = over.astype(qsend.dtype)
            send(PY, n, qsend, qgot, to_y)

    def parent_own(n):
        if n < last:
            got(PY, n, pygot.at[n], to_y)
            came = pygot[n]
        else:
            got(PY, n, qgot, to_y)
            came = qgot[...].astype(jnp.float32)
        own = pbuf[n, y, core] + pgot[n, y] + came
        pv[n] = own
        esend[n] = own.astype(esend.dtype)
        send(PZ, n, esend.at[n], egot.at[n], to_z)

    def parent_all(n):
        got(PZ, n, egot.at[n], to_z)
        pv[n] = pv[n] + egot[n].astype(jnp.float32)
        one = pltpu.make_async_copy(pv.at[n], out_ref.at[1, n], out_sem.at[1, n])
        one.start()
        outs.append(one)

    r_in.wait()
    k_in.wait()
    for n in range(nodes):
        relay(n)
    eliminate(0)
    reduce_chip(0)
    send(LY, last, l_ref.at[last, pl.ds(0, half)], piece(last, 2, 0), to_y)
    send(MY, last, l_ref.at[last, pl.ds(half, rest)], piece(last, 2, half), to_y)
    for n in range(nodes):
        got(TZ, n, strip(zw, n, c), to_z)
        send(ZC, n, strip(zw, n, c), strip(zw, n, c), to_core)
    for n in range(1, last):
        eliminate(n)
        reduce_chip(n)

    def hand_on(n):
        got(TG, n, strip(zw, n, yp), to_z)
        send(ZG, n, strip(zw, n, yp), strip(zw, n, yp), to_core)

    hand_on(0)
    couple(0)
    merge(0)
    total = begin(last)
    parent_chip(0)
    got(LY, last, piece(last, 2, 0), to_y)
    send(LF, last, piece(last, 2, 0), piece(last, 3, 0), to_core)
    total = total + times(last, 2 * block, half)
    for n in range(1, last):
        hand_on(n)
    got(LF, last, piece(last, 3, 0), to_core)
    total = total + times(last, 3 * block, half)
    got(MY, last, piece(last, 2, half), to_y)
    send(MF, last, piece(last, 2, half), piece(last, 3, half), to_core)
    total = total + times(last, 2 * block + half, rest)
    for n in range(1, last):
        couple(n)
    got(MF, last, piece(last, 3, half), to_core)
    total = total + times(last, 3 * block + half, rest)
    skeletons(last, total)
    for n in range(1, last):
        merge(n)
    reduce_chip(last)
    for n in range(1, last):
        parent_chip(n)
    parent_own(0)
    hand_on(last)
    couple(last)
    merge(last)
    for n in range(1, last):
        parent_own(n)
    parent_chip(last)
    parent_all(0)
    parent_own(last)
    for n in range(1, last):
        parent_all(n)
    parent_all(last)
    for one in sent:
        one.wait_send()
    for one in outs:
        one.wait()


def shards(diagonal_inverses, column_basis, row_basis, transfer, coupling, ranks):
    nodes, block, whole = diagonal_inverses.shape
    part, width = transfer.shape[1:]
    f32, bf16 = jnp.float32, jnp.bfloat16
    skeleton_link, parent_link, sibling_link = bf16, f32, bf16
    anywhere = pl.BlockSpec(memory_space=pl.ANY)
    strips = (nodes, part, width)
    square = (nodes, width, width)
    quads = (nodes, 2, 2, part, width)
    pairs = (nodes, 2, part, width)
    out = pl.pallas_call(
        kernel,
        out_shape=jax.ShapeDtypeStruct((2,) + strips, f32),
        in_specs=[pl.BlockSpec(memory_space=pltpu.SMEM)] + [anywhere] * 5,
        out_specs=anywhere,
        scratch_shapes=[
            pltpu.VMEM((nodes, block, whole), bf16),
            pltpu.VMEM((nodes, whole, width), bf16),
            pltpu.VMEM((nodes, block, width), bf16),
            pltpu.VMEM(strips, f32),
            pltpu.VMEM(strips, f32),
            pltpu.VMEM(square, f32),
            pltpu.VMEM(square, f32),
            pltpu.VMEM(quads, f32),
            pltpu.VMEM(pairs, f32),
            pltpu.VMEM(strips, skeleton_link),
            pltpu.VMEM(strips, skeleton_link),
            pltpu.VMEM(quads, f32),
            pltpu.VMEM(pairs, f32),
            pltpu.VMEM(strips, parent_link),
            pltpu.VMEM(strips, parent_link),
            pltpu.VMEM((part, width), bf16),
            pltpu.VMEM((part, width), bf16),
            pltpu.VMEM(strips, sibling_link),
            pltpu.VMEM(strips, sibling_link),
            pltpu.VMEM(strips, f32),
            pltpu.VMEM(strips, f32),
            pltpu.SemaphoreType.DMA((17, nodes)),
            pltpu.SemaphoreType.DMA((17, nodes)),
            pltpu.SemaphoreType.DMA((nodes, 5)),
            pltpu.SemaphoreType.DMA((3,)),
            pltpu.SemaphoreType.DMA((2, nodes)),
        ],
        compiler_params=pltpu.CompilerParams(collective_id=0, has_side_effects=True),
    )(ranks, diagonal_inverses, column_basis, row_basis, transfer, coupling)
    return out[0], out[1]


def solution(mesh):
    placed = (P("row", "col", None),) * 5 + (P("row"),)
    return jax.shard_map(
        shards,
        mesh=mesh,
        in_specs=placed,
        out_specs=(P("row", "col", None), P("row", "col", None)),
        check_vma=False,
    )
```

profile of v0, /device:TPU:0, one launch (start us, length us, event | category | flops | bytes accessed | tf_op | source)
XLA Modules:
  0.0 46.4 jit_solution(880408161094824522)
XLA Ops:
  0.6 43.9 %shard_map.77 = f32[2,3,64,256]{3,2,1,0:T(8,128)} custom-call(s32[3]{0:T(128)} %ranks_ref.1, bf16[3,512,2048]{2,1,0:T(8,128)(2,1)} %d_ref.1, bf16[3,512,256]{2,1,0:T(8,128)(2,1)} %l_ref.1, bf16[3,512,256]{2,1,0:T(8,128)(2,1)} %r_ref.1, f32[3,64,256]{2,1,0:T(8,128)} %t_ref.1, f32[3,64,256]{2,1,0:T(8,128)} %k_ref.1), custom_call_target="tpu_custom_call" | custom-call | tf_op jit(solution)/shard_map/pallas_call | solution.py:280
  44.6 1.8 %slice_bitcast_fusion = (f32[3,64,256]{2,1,0:T(8,128)}, f32[3,64,256]{2,1,0:T(8,128)}) fusion(f32[2,3,64,256]{3,2,1,0:T(8,128)} %shard_map.77), kind=kLoop, calls=%fused_computation | loop fusion | bytes 786432 | tf_op jit(solution)/shard_map/squeeze | solution.py:315
where the time goes:
time: 46.5 us; the launch traced here: 46.4 us
  Pallas kernels  43.9 us (94%)
  local copies, waits for them, and re-layouts  1.8 us (4%)
  between operations  0.64 us (1%)
    pallas_call x1, Pallas kernels, shards(): pl.pallas_call(kernel, out_shape=jax.ShapeDtypeStruct((2,) + strips, f32)...  43.9 us
    squeeze x1, local copies, waits for them, and re-layouts, shards(): return (out[0], out[1])  1.8 us

commit v1 on v0

v1 whole, which is shorter than its diff:
```python
import jax
import jax.numpy as jnp
from jax import lax
from jax.experimental import pallas as pl
from jax.experimental.pallas import tpu as pltpu
from jax.sharding import PartitionSpec as P

BIT = 2
MESH = pl.DeviceIdType.MESH
LC, TY, TC, TF, TZ, TG, ZC, ZG, SC, SY, PC, PY, PZ, PD = range(14)
KINDS = 14
PIECES = 4


def kernel(
    ranks_ref, d_ref, l_ref, r_ref, t_ref, k_ref, out_ref,
    dv, lv, rv, tv, kv, tb, zb, rt, mt, xb, sbuf, sgot, ysend, ygot, pbuf, pgot,
    own_send, over_send, yin, zin, din, mv, pv,
    send_sem, recv_sem, ly_send, ly_recv, lf_send, lf_recv, d_sem, loc_sem, out_sem,
):
    nodes, block, _ = l_ref.shape
    part = t_ref.shape[1]
    width = t_ref.shape[2]
    f32, bf16 = jnp.float32, jnp.bfloat16
    c = lax.axis_index("col")
    r = lax.axis_index("row")
    core = lax.rem(c, 2)
    y = lax.div(c, 2)
    cp = c + 1 - 2 * core
    yp = c + 2 - 4 * y
    dg = cp + yp - c
    high = lax.rem(lax.div(r, 1 << BIT), 2)
    sib = r + (1 << BIT) - (2 << BIT) * high
    other = 1 - y
    last = nodes - 1

    to_core = {"col": cp}
    to_y = {"col": yp}
    to_z = {"row": sib}
    to_d = {"row": sib, "col": yp}
    slots = (c, cp, yp, dg)

    barrier = pltpu.get_barrier_semaphore()
    for device in (to_z, to_d, to_y, to_core):
        pl.semaphore_signal(barrier, inc=1, device_id=device, device_id_type=MESH)

    t_in = pltpu.make_async_copy(t_ref, tv, loc_sem.at[0])
    t_in.start()
    l_in, d_in = [], []
    for n in range(nodes):
        one = pltpu.make_async_copy(l_ref.at[n], lv.at[n, pl.ds(0, block)], d_sem.at[n, 4])
        one.start()
        l_in.append(one)
        for s in range(4):
            src = d_ref.at[n, :, pl.ds(pl.multiple_of(slots[s] * block, block), block)]
            one = pltpu.make_async_copy(src, dv.at[n, :, pl.ds(s * block, block)], d_sem.at[n, s])
            one.start()
            d_in.append(one)
        if n == 0:
            r_in = pltpu.make_async_copy(r_ref, rv, loc_sem.at[1])
            r_in.start()
    k_in = pltpu.make_async_copy(k_ref, kv, loc_sem.at[2])
    k_in.start()

    sent = []

    def remote(sems, src, dst, device):
        return pltpu.make_async_remote_copy(
            src_ref=src, dst_ref=dst, send_sem=sems[0], recv_sem=sems[1],
            device_id=device, device_id_type=MESH,
        )

    def of(kind, n):
        return send_sem.at[kind, n], recv_sem.at[kind, n]

    def send(kind, n, src, dst, device):
        one = remote(of(kind, n), src, dst, device)
        one.start()
        sent.append(one)

    def got(kind, n, ref, device):
        remote(of(kind, n), ref, ref, device).wait_recv()

    def halves(x):
        top = x.astype(bf16)
        return top, (x - top.astype(f32)).astype(bf16)

    def square(buf, n, level):
        return buf[n, :, level].reshape(width, width)

    def times_full(x, buf, n):
        top, low = halves(x)
        lhs = jnp.concatenate([top, low, top], axis=1)
        b_top, b_low = square(buf, n, 0), square(buf, n, 1)
        rhs = jnp.concatenate([b_top, b_top, b_low], axis=0)
        return jnp.dot(lhs, rhs, preferred_element_type=f32)

    def cuts(n):
        half, quarter = block // 2, block // 4
        if n < last:
            return ((0, half), (half, block - half))
        return ((0, half), (half, quarter), (half + quarter, block - half - quarter))

    def piece(n, s, cut):
        return lv.at[n, pl.ds(s * block + cut[0], cut[1])]

    def send_basis(n):
        for i, cut in enumerate(cuts(n)):
            one = remote(
                (ly_send.at[n, i], ly_recv.at[n, i]),
                l_ref.at[n, pl.ds(cut[0], cut[1])], piece(n, 2, cut), to_y,
            )
            one.start()
            sent.append(one)

    def send_core(n):
        send(LC, n, l_ref.at[n], lv.at[n, pl.ds(block, block)], to_core)

    row_at = lax.broadcasted_iota(jnp.int32, (part, width), 0) + c * part
    col_at = lax.broadcasted_iota(jnp.int32, (part, width), 1)
    zeros = jnp.zeros((part, width), bf16)

    pl.semaphore_wait(barrier, 4)
    send_basis(0)
    send_core(0)
    t_in.wait()
    for n in range(nodes):
        top, low = halves(jnp.where(row_at < ranks_ref[n], tv[n], 0.0))
        tb[n, c, 0] = top
        tb[n, c, 1] = low
        for buf in (tb, zb):
            for strip in (yp, dg):
                buf[n, strip, 1] = zeros
    for n in range(nodes):
        send(TZ, n, tb.at[n, c], zb.at[n, c], to_z)
        send(TY, n, tb.at[n, c, 0], tb.at[n, c, 0], to_y)
        send(TC, n, tb.at[n, c], tb.at[n, c], to_core)
    for n in range(1, nodes):
        send_basis(n)
        send_core(n)

    def times(n, first, size):
        span = pl.ds(first, size)
        return jnp.dot(dv[n, :, span], lv[n, span, :], preferred_element_type=f32)

    def begin(n):
        l_in[n].wait()
        for s in range(4):
            d_in[4 * n + s].wait()
        got(LC, n, lv.at[n, pl.ds(block, block)], to_core)
        return times(n, 0, 2 * block)

    def eliminate(n, total):
        before = None
        for i, cut in enumerate(cuts(n)):
            mine = piece(n, 2, cut)
            remote((ly_send.at[n, i], ly_recv.at[n, i]), mine, mine, to_y).wait_recv()
            one = remote((lf_send.at[n, i], lf_recv.at[n, i]), mine, piece(n, 3, cut), to_core)
            one.start()
            sent.append(one)
            total = total + times(n, 2 * block + cut[0], cut[1])
            theirs = piece(n, 3, cut)
            remote((lf_send.at[n, i], lf_recv.at[n, i]), theirs, theirs, to_core).wait_recv()
            total = total + times(n, 3 * block + cut[0], cut[1])
        return total

    def skeletons(n, total):
        skeleton = jnp.dot(rt[n], total.astype(bf16), preferred_element_type=f32)
        sbuf[n] = skeleton.reshape(2, 2, part, width)
        send(SC, n, sbuf.at[n, :, 1 - core], sgot.at[n], to_core)

    def reduce_chip(n):
        got(SC, n, sgot.at[n], to_core)
        ysend[n] = (sbuf[n, other, core] + sgot[n, other]).astype(ysend.dtype)
        send(SY, n, ysend.at[n], ygot.at[n], to_y)

    def relay(n):
        got(TY, n, tb.at[n, yp, 0], to_y)
        send(TG, n, tb.at[n, yp, 0], zb.at[n, yp, 0], to_z)
        send(TF, n, tb.at[n, yp, 0], tb.at[n, yp, 0], to_core)

    def spread(n):
        got(TZ, n, zb.at[n, c], to_z)
        send(ZC, n, zb.at[n, c], zb.at[n, c], to_core)

    def hand_on(n):
        got(TG, n, zb.at[n, yp, 0], to_z)
        send(ZG, n, zb.at[n, yp, 0], zb.at[n, yp, 0], to_core)

    def whole_transfer(n):
        got(TC, n, tb.at[n, cp], to_core)
        got(TF, n, tb.at[n, dg, 0], to_core)
        top, low = square(tb, n, 0).T, square(tb, n, 1).T
        mt[n, :, pl.ds(0, width)] = top
        mt[n, :, pl.ds(width, width)] = low
        mt[n, :, pl.ds(2 * width, width)] = top

    def couple(n):
        got(ZC, n, zb.at[n, cp], to_core)
        got(ZG, n, zb.at[n, dg, 0], to_core)
        mv[n] = times_full(kv[n], zb, n)

    def partial(n):
        xb[...] = times_full(sbuf[n].reshape(width, width), tb, n).reshape(4, part, width)
        xb[c] = xb[c] + mv[n]
        top, low = halves(xb[...].reshape(width, width))
        rhs = jnp.concatenate([top, top, low], axis=0)
        own = jnp.dot(mt[n], rhs, preferred_element_type=f32)
        pbuf[n] = own.reshape(2, 2, part, width)
        send(PC, n, pbuf.at[n, :, 1 - core], pgot.at[n], to_core)

    def parent_send(n):
        got(PC, n, pgot.at[n], to_core)
        over = (pbuf[n, other, core] + pgot[n, other]).astype(bf16)
        own = pbuf[n, y, core] + pgot[n, y]
        over_send[n] = over
        send(PD, n, over_send.at[n], din.at[n], to_d)
        own_send[n] = own.astype(bf16)
        send(PZ, n, own_send.at[n], zin.at[n], to_z)
        send(PY, n, over_send.at[n], yin.at[n], to_y)
        pv[n] = own

    outs = []

    def store(which, n, ref):
        one = pltpu.make_async_copy(ref.at[n], out_ref.at[which, n], out_sem.at[which, n])
        one.start()
        outs.append(one)

    def merge(n):
        got(SY, n, ygot.at[n], to_y)
        mine = sbuf[n, y, core] + sgot[n, y] + ygot[n].astype(f32)
        live = (row_at < ranks_ref[n]) & (col_at < ranks_ref[n])
        mv[n] = mv[n] + times_full(jnp.where(live, mine, 0.0), tb, n)
        store(0, n, mv)

    def parent_all(n):
        got(PY, n, yin.at[n], to_y)
        got(PZ, n, zin.at[n], to_z)
        got(PD, n, din.at[n], to_d)
        pv[n] = (pv[n] + yin[n].astype(f32)) + (zin[n].astype(f32) + din[n].astype(f32))
        store(1, n, pv)

    r_in.wait()
    for n in range(nodes):
        rt[n] = rv[n].T
    skeletons(0, eliminate(0, begin(0)))
    for n in range(nodes):
        relay(n)
    for n in range(nodes):
        spread(n)
    reduce_chip(0)
    for n in range(nodes):
        whole_transfer(n)
    k_in.wait()
    for n in range(1, last):
        skeletons(n, eliminate(n, begin(n)))
    total = begin(last)
    for n in range(1, last):
        reduce_chip(n)
    for n in range(nodes):
        hand_on(n)
    for n in range(nodes):
        couple(n)
    for n in range(last):
        partial(n)
    for n in range(last):
        parent_send(n)
    skeletons(last, eliminate(last, total))
    partial(last)
    reduce_chip(last)
    parent_send(last)
    for n in range(last):
        merge(n)
        parent_all(n)
    merge(last)
    parent_all(last)
    for one in sent:
        one.wait_send()
    for one in outs:
        one.wait()


def shards(diagonal_inverses, column_basis, row_basis, transfer, coupling, ranks):
    nodes, block, whole = diagonal_inverses.shape
    part, width = transfer.shape[1:]
    f32, bf16 = jnp.float32, jnp.bfloat16
    anywhere = pl.BlockSpec(memory_space=pl.ANY)
    strips = (nodes, part, width)
    quads = (nodes, 2, 2, part, width)
    pairs = (nodes, 2, part, width)
    vmem = pltpu.VMEM
    dma = pltpu.SemaphoreType.DMA
    out = pl.pallas_call(
        kernel,
        out_shape=jax.ShapeDtypeStruct((2,) + strips, f32),
        in_specs=[pl.BlockSpec(memory_space=pltpu.SMEM)] + [anywhere] * 5,
        out_specs=anywhere,
        scratch_shapes=[
            vmem((nodes, block, whole), bf16),
            vmem((nodes, whole, width), bf16),
            vmem((nodes, block, width), bf16),
            vmem(strips, f32),
            vmem(strips, f32),
            vmem((nodes, 4, 2, part, width), bf16),
            vmem((nodes, 4, 2, part, width), bf16),
            vmem((nodes, width, block), bf16),
            vmem((nodes, width, 3 * width), bf16),
            vmem((4, part, width), f32),
            vmem(quads, f32),
            vmem(pairs, f32),
            vmem(strips, bf16),
            vmem(strips, bf16),
            vmem(quads, f32),
            vmem(pairs, f32),
            vmem(strips, bf16),
            vmem(strips, bf16),
            vmem(strips, bf16),
            vmem(strips, bf16),
            vmem(strips, bf16),
            vmem(strips, f32),
            vmem(strips, f32),
            dma((KINDS, nodes)),
            dma((KINDS, nodes)),
            dma((nodes, PIECES)),
            dma((nodes, PIECES)),
            dma((nodes, PIECES)),
            dma((nodes, PIECES)),
            dma((nodes, 5)),
            dma((3,)),
            dma((2, nodes)),
        ],
        compiler_params=pltpu.CompilerParams(collective_id=0, has_side_effects=True),
    )(ranks, diagonal_inverses, column_basis, row_basis, transfer, coupling)
    return out[0], out[1]


def solution(mesh):
    placed = (P("row", "col", None),) * 5 + (P("row"),)
    return jax.shard_map(
        shards,
        mesh=mesh,
        in_specs=placed,
        out_specs=(P("row", "col", None), P("row", "col", None)),
        check_vma=False,
    )
```

time: 46.5 us -> 43.1 us (0.927)
  Pallas kernels: 43.9 us -> 40.5 us
    pallas_call x1, Pallas kernels: 43.9 us -> 40.5 us  [shards(): pl.pallas_call(kernel, out_shape=jax.ShapeDtypeStruct((2,) + strips, f32)...]
where the time goes in v1:
time: 43.1 us; the launch traced here: 43 us
  Pallas kernels  40.5 us (94%)
  local copies, waits for them, and re-layouts  1.8 us (4%)
  between operations  0.64 us (1%)
    pallas_call x1, Pallas kernels, shards(): pl.pallas_call(kernel, out_shape=jax.ShapeDtypeStruct((2,) + strips, f32)...  40.5 us
    squeeze x1, local copies, waits for them, and re-layouts, shards(): return (out[0], out[1])  1.8 us

profile of v1, /device:TPU:0, one launch (start us, length us, event | category | flops | bytes accessed | tf_op | source)
XLA Modules:
  0.0 43.0 jit_solution(8782852020280917596)
XLA Ops:
  0.6 40.5 %shard_map.77 = f32[2,3,64,256]{3,2,1,0:T(8,128)} custom-call(s32[3]{0:T(128)} %ranks_ref.1, bf16[3,512,2048]{2,1,0:T(8,128)(2,1)} %d_ref.1, bf16[3,512,256]{2,1,0:T(8,128)(2,1)} %l_ref.1, bf16[3,512,256]{2,1,0:T(8,128)(2,1)} %r_ref.1, f32[3,64,256]{2,1,0:T(8,128)} %t_ref.1, f32[3,64,256]{2,1,0:T(8,128)} %k_ref.1), custom_call_target="tpu_custom_call" | custom-call | tf_op jit(solution)/shard_map/pallas_call | solution.py:294
  41.2 1.8 %slice_bitcast_fusion = (f32[3,64,256]{2,1,0:T(8,128)}, f32[3,64,256]{2,1,0:T(8,128)}) fusion(f32[2,3,64,256]{3,2,1,0:T(8,128)} %shard_map.77), kind=kLoop, calls=%fused_computation | loop fusion | bytes 786432 | tf_op jit(solution)/shard_map/squeeze | solution.py:335

commit v2 on v1

--- a/solution.py
+++ b/solution.py
@@ -15,7 +15,7 @@
 def kernel(
     ranks_ref, d_ref, l_ref, r_ref, t_ref, k_ref, out_ref,
     dv, lv, rv, tv, kv, tb, zb, rt, mt, xb, sbuf, sgot, ysend, ygot, pbuf, pgot,
-    own_send, over_send, yin, zin, din, mv, pv,
+    own_send, over_full, over_send, yin, zin, din, mv, pv,
     send_sem, recv_sem, ly_send, ly_recv, lf_send, lf_recv, d_sem, loc_sem, out_sem,
 ):
     nodes, block, _ = l_ref.shape
@@ -150,19 +150,37 @@
         got(LC, n, lv.at[n, pl.ds(block, block)], to_core)
         return times(n, 0, 2 * block)
 
-    def eliminate(n, total):
-        before = None
-        for i, cut in enumerate(cuts(n)):
-            mine = piece(n, 2, cut)
-            remote((ly_send.at[n, i], ly_recv.at[n, i]), mine, mine, to_y).wait_recv()
-            one = remote((lf_send.at[n, i], lf_recv.at[n, i]), mine, piece(n, 3, cut), to_core)
-            one.start()
-            sent.append(one)
-            total = total + times(n, 2 * block + cut[0], cut[1])
-            theirs = piece(n, 3, cut)
-            remote((lf_send.at[n, i], lf_recv.at[n, i]), theirs, theirs, to_core).wait_recv()
-            total = total + times(n, 3 * block + cut[0], cut[1])
-        return total
+    totals = {}
+
+    def start(n):
+        totals[n] = begin(n)
+
+    def pass_on(n, i):
+        mine = piece(n, 2, cuts(n)[i])
+        remote((ly_send.at[n, i], ly_recv.at[n, i]), mine, mine, to_y).wait_recv()
+        one = remote((lf_send.at[n, i], lf_recv.at[n, i]), mine, piece(n, 3, cuts(n)[i]), to_core)
+        one.start()
+        sent.append(one)
+
+    def far(n, i):
+        cut = cuts(n)[i]
+        totals[n] = totals[n] + times(n, 2 * block + cut[0], cut[1])
+
+    def near(n, i):
+        cut = cuts(n)[i]
+        theirs = piece(n, 3, cut)
+        remote((lf_send.at[n, i], lf_recv.at[n, i]), theirs, theirs, to_core).wait_recv()
+        totals[n] = totals[n] + times(n, 3 * block + cut[0], cut[1])
+
+    def finish(n):
+        skeletons(n, totals[n])
+
+    def right(n):
+        rt[n] = rv[n].T
+
+    def waits(n):
+        r_in.wait()
+        k_in.wait()
 
     def skeletons(n, total):
         skeleton = jnp.dot(rt[n], total.astype(bf16), preferred_element_type=f32)
@@ -211,13 +229,14 @@
 
     def parent_send(n):
         got(PC, n, pgot.at[n], to_core)
-        over = (pbuf[n, other, core] + pgot[n, other]).astype(bf16)
+        over = pbuf[n, other, core] + pgot[n, other]
         own = pbuf[n, y, core] + pgot[n, y]
-        over_send[n] = over
+        over_full[n] = over
+        over_send[n] = over.astype(bf16)
         send(PD, n, over_send.at[n], din.at[n], to_d)
         own_send[n] = own.astype(bf16)
         send(PZ, n, own_send.at[n], zin.at[n], to_z)
-        send(PY, n, over_send.at[n], yin.at[n], to_y)
+        send(PY, n, over_full.at[n], yin.at[n], to_y)
         pv[n] = own
 
     outs = []
@@ -238,43 +257,70 @@
         got(PY, n, yin.at[n], to_y)
         got(PZ, n, zin.at[n], to_z)
         got(PD, n, din.at[n], to_d)
-        pv[n] = (pv[n] + yin[n].astype(f32)) + (zin[n].astype(f32) + din[n].astype(f32))
+        pv[n] = (pv[n] + yin[n]) + (zin[n].astype(f32) + din[n].astype(f32))
         store(1, n, pv)
 
-    r_in.wait()
-    for n in range(nodes):
-        rt[n] = rv[n].T
-    skeletons(0, eliminate(0, begin(0)))
-    for n in range(nodes):
-        relay(n)
-    for n in range(nodes):
-        spread(n)
+    start(0)
+    waits(0)
+    right(0)
+    right(1)
+    right(2)
+    start(1)
+    start(2)
+    pass_on(0, 0)
+    far(0, 0)
+    near(0, 0)
+    pass_on(0, 1)
+    far(0, 1)
+    near(0, 1)
+    finish(0)
+    relay(0)
+    relay(1)
+    relay(2)
+    spread(0)
+    spread(1)
+    spread(2)
     reduce_chip(0)
-    for n in range(nodes):
-        whole_transfer(n)
-    k_in.wait()
-    for n in range(1, last):
-        skeletons(n, eliminate(n, begin(n)))
-    total = begin(last)
-    for n in range(1, last):
-        reduce_chip(n)
-    for n in range(nodes):
-        hand_on(n)
-    for n in range(nodes):
-        couple(n)
-    for n in range(last):
-        partial(n)
-    for n in range(last):
-        parent_send(n)
-    skeletons(last, eliminate(last, total))
-    partial(last)
-    reduce_chip(last)
-    parent_send(last)
-    for n in range(last):
-        merge(n)
-        parent_all(n)
-    merge(last)
-    parent_all(last)
+    whole_transfer(0)
+    whole_transfer(1)
+    whole_transfer(2)
+    pass_on(1, 0)
+    far(1, 0)
+    near(1, 0)
+    pass_on(1, 1)
+    far(1, 1)
+    hand_on(0)
+    hand_on(1)
+    hand_on(2)
+    near(1, 1)
+    finish(1)
+    couple(0)
+    partial(0)
+    couple(1)
+    partial(1)
+    reduce_chip(1)
+    pass_on(2, 0)
+    far(2, 0)
+    couple(2)
+    near(2, 0)
+    parent_send(0)
+    pass_on(2, 1)
+    far(2, 1)
+    parent_send(1)
+    near(2, 1)
+    pass_on(2, 2)
+    far(2, 2)
+    near(2, 2)
+    finish(2)
+    partial(2)
+    reduce_chip(2)
+    parent_send(2)
+    merge(0)
+    merge(1)
+    parent_all(0)
+    parent_all(1)
+    merge(2)
+    parent_all(2)
     for one in sent:
         one.wait_send()
     for one in outs:
@@ -314,8 +360,9 @@
             vmem(quads, f32),
             vmem(pairs, f32),
             vmem(strips, bf16),
-            vmem(strips, bf16),
-            vmem(strips, bf16),
+            vmem(strips, f32),
+            vmem(strips, bf16),
+            vmem(strips, f32),
             vmem(strips, bf16),
             vmem(strips, bf16),
             vmem(strips, f32),

time: 43.1 us -> 41 us (0.951)
  Pallas kernels: 40.5 us -> 38.4 us
    pallas_call x1, Pallas kernels: 40.5 us -> 38.4 us  [shards(): pl.pallas_call(kernel, out_shape=jax.ShapeDtypeStruct((2,) + strips, f32)...]
where the time goes in v2:
time: 41 us; the launch traced here: 40.8 us
  Pallas kernels  38.4 us (94%)
  local copies, waits for them, and re-layouts  1.8 us (4%)
  between operations  0.64 us (2%)
    pallas_call x1, Pallas kernels, shards(): pl.pallas_call(kernel, out_shape=jax.ShapeDtypeStruct((2,) + strips, f32)...  38.4 us
    squeeze x1, local copies, waits for them, and re-layouts, shards(): return (out[0], out[1])  1.8 us

profile of v2, /device:TPU:0, one launch (start us, length us, event | category | flops | bytes accessed | tf_op | source)
XLA Modules:
  0.0 40.8 jit_solution(3695207545138674207)
XLA Ops:
  0.6 38.4 %shard_map.77 = f32[2,3,64,256]{3,2,1,0:T(8,128)} custom-call(s32[3]{0:T(128)} %ranks_ref.1, bf16[3,512,2048]{2,1,0:T(8,128)(2,1)} %d_ref.1, bf16[3,512,256]{2,1,0:T(8,128)(2,1)} %l_ref.1, bf16[3,512,256]{2,1,0:T(8,128)(2,1)} %r_ref.1, f32[3,64,256]{2,1,0:T(8,128)} %t_ref.1, f32[3,64,256]{2,1,0:T(8,128)} %k_ref.1), custom_call_target="tpu_custom_call" | custom-call | tf_op jit(solution)/shard_map/pallas_call | solution.py:340
  39.0 1.8 %slice_bitcast_fusion = (f32[3,64,256]{2,1,0:T(8,128)}, f32[3,64,256]{2,1,0:T(8,128)}) fusion(f32[2,3,64,256]{3,2,1,0:T(8,128)} %shard_map.77), kind=kLoop, calls=%fused_computation | loop fusion | bytes 786432 | tf_op jit(solution)/shard_map/squeeze | solution.py:382

commit v3 on v2

--- a/solution.py
+++ b/solution.py
@@ -47,7 +47,8 @@
     t_in = pltpu.make_async_copy(t_ref, tv, loc_sem.at[0])
     t_in.start()
     l_in, d_in = [], []
-    for n in range(nodes):
+
+    def load(n):
         one = pltpu.make_async_copy(l_ref.at[n], lv.at[n, pl.ds(0, block)], d_sem.at[n, 4])
         one.start()
         l_in.append(one)
@@ -56,12 +57,12 @@
             one = pltpu.make_async_copy(src, dv.at[n, :, pl.ds(s * block, block)], d_sem.at[n, s])
             one.start()
             d_in.append(one)
-        if n == 0:
-            r_in = pltpu.make_async_copy(r_ref, rv, loc_sem.at[1])
-            r_in.start()
+
+    load(0)
+    r_in = pltpu.make_async_copy(r_ref, rv, loc_sem.at[1])
+    r_in.start()
     k_in = pltpu.make_async_copy(k_ref, kv, loc_sem.at[2])
     k_in.start()
-
     sent = []
 
     def remote(sems, src, dst, device):
@@ -138,6 +139,9 @@
     for n in range(1, nodes):
         send_basis(n)
         send_core(n)
+
+    for n in range(1, nodes):
+        load(n)
 
     def times(n, first, size):
         span = pl.ds(first, size)
@@ -298,15 +302,15 @@
     partial(0)
     couple(1)
     partial(1)
+    parent_send(0)
     reduce_chip(1)
     pass_on(2, 0)
+    parent_send(1)
     far(2, 0)
     couple(2)
     near(2, 0)
-    parent_send(0)
     pass_on(2, 1)
     far(2, 1)
-    parent_send(1)
     near(2, 1)
     pass_on(2, 2)
     far(2, 2)

time: 41 us -> 40.5 us (0.988)
  Pallas kernels: 38.4 us -> 37.9 us
    pallas_call x1, Pallas kernels: 38.4 us -> 37.9 us  [shards(): pl.pallas_call(kernel, out_shape=jax.ShapeDtypeStruct((2,) + strips, f32)...]
where the time goes in v3:
time: 40.5 us; the launch traced here: 40.3 us
  Pallas kernels  37.9 us (94%)
  local copies, waits for them, and re-layouts  1.8 us (4%)
  between operations  0.64 us (2%)
    pallas_call x1, Pallas kernels, shards(): pl.pallas_call(kernel, out_shape=jax.ShapeDtypeStruct((2,) + strips, f32)...  37.9 us
    squeeze x1, local copies, waits for them, and re-layouts, shards(): return (out[0], out[1])  1.8 us

profile of v3, /device:TPU:0, one launch (start us, length us, event | category | flops | bytes accessed | tf_op | source)
XLA Modules:
  0.0 40.3 jit_solution(1724730987252171135)
XLA Ops:
  0.6 37.9 %shard_map.77 = f32[2,3,64,256]{3,2,1,0:T(8,128)} custom-call(s32[3]{0:T(128)} %ranks_ref.1, bf16[3,512,2048]{2,1,0:T(8,128)(2,1)} %d_ref.1, bf16[3,512,256]{2,1,0:T(8,128)(2,1)} %l_ref.1, bf16[3,512,256]{2,1,0:T(8,128)(2,1)} %r_ref.1, f32[3,64,256]{2,1,0:T(8,128)} %t_ref.1, f32[3,64,256]{2,1,0:T(8,128)} %k_ref.1), custom_call_target="tpu_custom_call" | custom-call | tf_op jit(solution)/shard_map/pallas_call | solution.py:344
  38.5 1.8 %slice_bitcast_fusion = (f32[3,64,256]{2,1,0:T(8,128)}, f32[3,64,256]{2,1,0:T(8,128)}) fusion(f32[2,3,64,256]{3,2,1,0:T(8,128)} %shard_map.77), kind=kLoop, calls=%fused_computation | loop fusion | bytes 786432 | tf_op jit(solution)/shard_map/squeeze | solution.py:386

commit v4 on v3

--- a/solution.py
+++ b/solution.py
@@ -227,9 +227,14 @@
         xb[c] = xb[c] + mv[n]
         top, low = halves(xb[...].reshape(width, width))
         rhs = jnp.concatenate([top, top, low], axis=0)
-        own = jnp.dot(mt[n], rhs, preferred_element_type=f32)
-        pbuf[n] = own.reshape(2, 2, part, width)
-        send(PC, n, pbuf.at[n, :, 1 - core], pgot.at[n], to_core)
+        for side in (1 - core, core):
+            lhs = jnp.concatenate(
+                [mt[n, pl.ds(pl.multiple_of((2 * half + side) * part, part), part)] for half in range(2)], axis=0
+            )
+            rows = jnp.dot(lhs, rhs, preferred_element_type=f32)
+            pbuf[n, :, side] = rows.reshape(2, part, width)
+            if side is not core:
+                send(PC, n, pbuf.at[n, :, 1 - core], pgot.at[n], to_core)
 
     def parent_send(n):
         got(PC, n, pgot.at[n], to_core)
@@ -291,23 +296,23 @@
     pass_on(1, 0)
     far(1, 0)
     near(1, 0)
+    hand_on(0)
+    hand_on(1)
+    couple(0)
+    partial(0)
     pass_on(1, 1)
     far(1, 1)
-    hand_on(0)
-    hand_on(1)
+    parent_send(0)
     hand_on(2)
+    couple(1)
     near(1, 1)
     finish(1)
-    couple(0)
-    partial(0)
-    couple(1)
     partial(1)
-    parent_send(0)
+    couple(2)
     reduce_chip(1)
+    parent_send(1)
     pass_on(2, 0)
-    parent_send(1)
     far(2, 0)
-    couple(2)
     near(2, 0)
     pass_on(2, 1)
     far(2, 1)

time: 40.5 us -> 40.2 us (level)
  no operation moved by 1% of the time
where the time goes in v4:
time: 40.2 us; the launch traced here: 40.1 us
  Pallas kernels  37.6 us (94%)
  local copies, waits for them, and re-layouts  1.8 us (4%)
  between operations  0.64 us (2%)
    pallas_call x1, Pallas kernels, shards(): pl.pallas_call(kernel, out_shape=jax.ShapeDtypeStruct((2,) + strips, f32)...  37.6 us
    squeeze x1, local copies, waits for them, and re-layouts, shards(): return (out[0], out[1])  1.8 us

profile of v4, /device:TPU:0, one launch (start us, length us, event | category | flops | bytes accessed | tf_op | source)
XLA Modules:
  0.0 40.1 jit_solution(3010243451695205780)
XLA Ops:
  0.6 37.6 %shard_map.77 = f32[2,3,64,256]{3,2,1,0:T(8,128)} custom-call(s32[3]{0:T(128)} %ranks_ref.1, bf16[3,512,2048]{2,1,0:T(8,128)(2,1)} %d_ref.1, bf16[3,512,256]{2,1,0:T(8,128)(2,1)} %l_ref.1, bf16[3,512,256]{2,1,0:T(8,128)(2,1)} %r_ref.1, f32[3,64,256]{2,1,0:T(8,128)} %t_ref.1, f32[3,64,256]{2,1,0:T(8,128)} %k_ref.1), custom_call_target="tpu_custom_call" | custom-call | tf_op jit(solution)/shard_map/pallas_call | solution.py:349
  38.3 1.8 %slice_bitcast_fusion = (f32[3,64,256]{2,1,0:T(8,128)}, f32[3,64,256]{2,1,0:T(8,128)}) fusion(f32[2,3,64,256]{3,2,1,0:T(8,128)} %shard_map.77), kind=kLoop, calls=%fused_computation | loop fusion | bytes 786432 | tf_op jit(solution)/shard_map/squeeze | solution.py:391
